TPU v7x, 32 devices: a whole 2x2x4 slice. The times are simulated.
32 devices in a mesh: band: 8 (over z, y), lev: 4 (over x, core).
Axes of the slice: x: 2, y: 2, z: 4, core: 2. Of those that a mesh axis runs over, the one named last changes fastest.
Arguments:
- grid_adjoint: float32 [1024, 64, 2048], P('band', 'lev'), may hold values from -6 to 6
- trajectory: float32 [1024, 64, 2048], P('band', 'lev'), may hold values from -3 to 3
- legendre_north: float32 [512, 512, 512], P(('band', 'lev')), may hold values from -0.25 to 0.25
- slot_wavenumber: int32 [512], replicated, may hold values from 0 to 511, each once
- spectral_state: float32 [512, 512, 2, 64], P(('band', 'lev')), may hold values from -6 to 6
- to_modes: float32 [64, 64], replicated, may hold values from -0.75 to 0.75
- from_modes: float32 [64, 64], replicated, may hold values from -0.75 to 0.75
- rates: float32 [64], replicated, may hold values from 0.1 to 10
Outputs:
- spectral_out: float32 [512, 512, 2, 64], P(('band', 'lev'))
- grid_out: float32 [1024, 64, 2048], P('band', 'lev')
Inputs may be any that keep to these rules, and one draw needn't show every extreme that they name: `slot_wavenumber`: each wavenumber stands in exactly one slot.
All inputs are finite; a program needn't handle non-finite values.
Results may differ from a plain program's by a relative error of at most 0.000067.
Values sent between devices are 32-bit elements; how exact they have to be, the bound alone decides.
A program may use at most 192 MiB of HBM per device.

v0:
```python
import jax
import jax.numpy as jnp
from jax import lax
from jax.sharding import PartitionSpec as P


def wave_table(longitudes, count):
    column = jnp.arange(longitudes, dtype=jnp.int32)
    numbers = jnp.arange(count, dtype=jnp.int32)
    phase = column[:, None] * numbers[None, :] % longitudes
    angles = phase.astype(jnp.float32) * (2.0 * jnp.pi / longitudes)
    scale = jnp.float32(longitudes) ** (-0.5)
    return jnp.concatenate([jnp.cos(angles), -jnp.sin(angles)], axis=1) * scale


def fold(data):
    half = data.shape[2] // 2
    north = data[:, :, :half]
    south = data[:, :, half:][:, :, ::-1]
    return (north + south, north - south)


def by_parity(even_part, odd_part):
    depth_index = jnp.arange(even_part.shape[1], dtype=jnp.int32)
    keep = (depth_index % 2 == 0)[None, :, None, None]
    return jnp.where(keep, even_part, odd_part)


def analyse(north_table, even, odd):
    highest = lax.Precision.HIGHEST
    even_part = jnp.einsum("skt,cstl->skcl", north_table, even, precision=highest)
    odd_part = jnp.einsum("skt,cstl->skcl", north_table, odd, precision=highest)
    return by_parity(even_part, odd_part)


def synthesise(north_table, coeffs):
    highest = lax.Precision.HIGHEST
    depth = north_table.shape[1]
    depth_index = jnp.arange(depth, dtype=jnp.int32)
    even_mask = (depth_index % 2 == 0).astype(jnp.float32)[None, :, None, None]
    even_coeffs = coeffs * even_mask
    odd_coeffs = coeffs - even_coeffs
    first = jnp.einsum("skt,skcl->cstl", north_table, even_coeffs, precision=highest)
    second = jnp.einsum("skt,skcl->cstl", north_table, odd_coeffs, precision=highest)
    north = first + second
    south = (first - second)[:, :, ::-1]
    return jnp.concatenate([north, south], axis=2)


def couple(analysed, state, wavenumbers, to_modes, from_modes, rates):
    highest = lax.Precision.HIGHEST
    depth = analysed.shape[1]
    depth_index = jnp.arange(depth, dtype=jnp.int32)
    valid = (depth_index[None, :] < depth - wavenumbers[:, None]).astype(jnp.float32)
    total = (analysed + state) * valid[:, :, None, None]
    degree = (wavenumbers[:, None] + depth_index[None, :]).astype(jnp.float32)
    helm = degree * (degree + 1.0) / (depth * (depth - 1.0))
    modes = jnp.einsum("skcl,pl->skcp", total, to_modes, precision=highest)
    scaled = modes / (1.0 + helm[:, :, None, None] * rates)
    return jnp.einsum("skcp,lp->skcl", scaled, from_modes, precision=highest)


def shards(
    grid_adjoint,
    trajectory,
    legendre_north,
    slot_wavenumber,
    spectral_state,
    to_modes,
    from_modes,
    rates,
):
    highest = lax.Precision.HIGHEST
    lat_rows, level_rows, longitudes = grid_adjoint.shape
    width = slot_wavenumber.shape[0]
    slot_rows = legendre_north.shape[0]
    bands = lax.axis_size("band")
    levels_count = lax.axis_size("lev")
    band_at = lax.axis_index("band")
    level_at = lax.axis_index("lev")
    table = wave_table(longitudes, width)
    counting = jnp.arange(width, dtype=jnp.int32)
    inverse = jnp.zeros((width,), jnp.int32).at[slot_wavenumber].set(counting)
    forced = grid_adjoint * (1.0 + trajectory)
    flat = forced.reshape(lat_rows * level_rows, longitudes)
    natural = lax.dot_general(
        table, flat, (((0,), (1,)), ((), ())), precision=highest, preferred_element_type=jnp.float32
    )
    natural = natural.reshape(2, width, lat_rows * level_rows)
    fourier = jnp.take(natural, slot_wavenumber, axis=1).reshape(2, width, lat_rows, level_rows)
    own_start = (band_at * levels_count + level_at) * slot_rows
    own_waves = lax.dynamic_slice_in_dim(slot_wavenumber, own_start, slot_rows)
    gathered = lax.all_to_all(
        lax.all_to_all(fourier, "band", split_axis=1, concat_axis=2, tiled=True),
        "lev",
        split_axis=1,
        concat_axis=3,
        tiled=True,
    )
    even, odd = fold(gathered)
    analysed = analyse(legendre_north, even, odd)
    spectral_out = couple(analysed, spectral_state, own_waves, to_modes, from_modes, rates)
    synthesised = synthesise(legendre_north, spectral_out)
    returned = lax.all_to_all(
        lax.all_to_all(synthesised, "band", split_axis=2, concat_axis=1, tiled=True),
        "lev",
        split_axis=3,
        concat_axis=1,
        tiled=True,
    )
    level_part = counting // (bands * slot_rows)
    band_part = counting // slot_rows % bands
    within = counting % slot_rows
    source_slot = band_part * (levels_count * slot_rows) + level_part * slot_rows + within
    arrival_of_slot = jnp.zeros((width,), jnp.int32).at[source_slot].set(counting)
    pick = jnp.take(arrival_of_slot, inverse, axis=0)
    ordered = jnp.take(returned.reshape(2, width, lat_rows * level_rows), pick, axis=1)
    coeff_rows = ordered.reshape(2 * width, lat_rows * level_rows)
    grid_out = lax.dot_general(
        coeff_rows,
        table,
        (((0,), (1,)), ((), ())),
        precision=highest,
        preferred_element_type=jnp.float32,
    )
    return (spectral_out, grid_out.reshape(lat_rows, level_rows, longitudes))


def solution(mesh):
    return jax.shard_map(
        shards,
        mesh=mesh,
        in_specs=(
            P("band", "lev", None),
            P("band", "lev", None),
            P(("band", "lev"), None, None),
            P(),
            P(("band", "lev"), None, None, None),
            P(),
            P(),
            P(),
        ),
        out_specs=(P(("band", "lev"), None, None, None), P("band", "lev", None)),
        check_vma=False,
    )
```

profile of v0, /device:TPU:0, one launch (start us, length us, event | category | flops | bytes accessed | tf_op | source)
XLA Modules:
  0.0 1142.6 jit_solution(12280588452169938446)
XLA Ops:
  0.7 16.5 %sine_negate_fusion = (f32[2048,512]{1,0:T(8,128)S(1)}, f32[2048,512]{1,0:T(8,128)S(1)}) fusion(), kind=kLoop, calls=%fused_computation.41 | loop fusion | flops 15728640 | bytes 8388608 | tf_op jit(solution)/shard_map/neg | solution.py:13
  17.2 1.9 copy-done.4
  20.4 4.9 fusion.10
  25.3 9.2 copy.79
  34.5 11.7 %add_multiply_fusion = f32[128,16,2048]{2,1,0:T(8,128)S(1)} fusion(f32[128,16,2048]{2,1,0:T(8,128)} %param.10, f32[128,16,2048]{2,1,0:T(8,128)} %param.11), kind=kLoop, calls=%fused_computation.13 | loop fusion | flops 8388608 | bytes 50331648 | tf_op jit(solution)/shard_map/mul | solution.py:84
  46.2 66.8 %fusion.57 = f32[2,512,2048]{2,1,0:T(8,128)} fusion(f32[2,512,2048]{2,1,0:T(8,128)} %bitcast.91, f32[2048,2048,1]{1,0,2:T(8,128)S(1)} %bitcast.89), kind=kOutput, calls=%fused_computation.99 | convolution fusion | flops 51539607552 | bytes 33554432 | tf_op jit(solution)/shard_map/dot_general | solution.py:86
  113.0 15.4 %copy.80 = f32[2,512,2048]{2,0,1:T(2,128)} copy(f32[2,512,2048]{2,1,0:T(8,128)} %fusion.57) | data formatting | bytes 16777216 | tf_op jit(solution)/shard_map/dot_general | solution.py:86
  128.5 22.7 %gather_fusion.1 = f32[512,2,2048]{2,1,0:T(2,128)} fusion(f32[2,512,2048]{2,0,1:T(2,128)} %copy.80, s32[1024]{0:T(1024)S(1)} %pad_clamp_fusion.2), kind=kCustom, calls=%fused_computation.clone | custom fusion | bytes 16779264 | tf_op jit(solution)/shard_map/jit(_take)/gather | solution.py:90
  151.2 8.5 select_bitcast_fusion.1
  159.7 13.1 %copy.81 = f32[2,512,2048]{1,2,0:T(8,128)} copy(f32[2,512,2048]{2,0,1:T(2,128)} %select_bitcast_fusion.1) | data formatting | bytes 16777216 | tf_op jit(solution)/shard_map/jit(_take)/select_n | solution.py:90
  172.8 10.8 copy.82
  183.6 190.4 %all_to_all.69 = f32[2,512,128,16]{2,3,0,1:T(8,128)S(1)} all-to-all(f32[2,512,128,16]{2,3,0,1:T(8,128)} %copy.82), channel_id=1, replica_groups=mesh['band'=8,'lev'=4] {'band'}, dimensions={1} | all-to-all | bytes 16777216 | tf_op jit(solution)/shard_map/all_to_all | solution.py:94
  373.9 4.6 copy.120
  378.5 6.2 all-to-all-start.1
  384.9 1.7 multiply_add_fusion
  386.7 91.2 %all-to-all-done.1 = f32[2,64,1024,16]{2,3,0,1:T(8,128)} async-done(((f32[2,64,1024,16]{2,3,0,1:T(8,128)}), f32[2,64,1024,16]{2,3,0,1:T(8,128)}, u32[]{:S(2)}, u32[]{:S(2)}) %all-to-all-start.1) | async-done | bytes 8388640 | tf_op jit(solution)/shard_map/all_to_all | solution.py:93
  477.8 4.2 copy.87
  482.1 3.4 copy-done.2
  485.4 2.5 slice.15
  487.9 7.4 rev.6
  495.4 4.7 slice_subtract_fusion
  500.0 21.0 %fusion.4 = f32[16,2,64,512]{3,2,1,0:T(8,128)S(1)} fusion(f32[16,512,512]{2,1,0:T(8,128)} %param.12, f32[2,16,512,64]{2,3,1,0:T(8,128)S(1)} %get-tuple-element.19), kind=kOutput, calls=%fused_computation.9 | convolution fusion | flops 6442450944 | bytes 25165824 | tf_op jit(solution)/shard_map/skt,cstl->skcl/dot_general | solution.py:32
  521.0 21.4 %fusion.6 = f32[16,2,64,512]{3,2,1,0:T(8,128)S(1)} fusion(f32[16,512,512]{2,1,0:T(8,128)} %param.12, f32[2,16,512,64]{2,3,1,0:T(8,128)S(1)} %get-tuple-element.20), kind=kOutput, calls=%fused_computation.11 | convolution fusion | flops 6442450944 | bytes 25165824 | tf_op jit(solution)/shard_map/skt,cstl->skcl/dot_general | solution.py:31
  542.5 7.9 fusion.16
  550.4 5.0 fusion.20
  555.4 16.0 %fusion = f32[16,2,64,512]{3,2,1,0:T(8,128)} fusion(f32[16,512,512]{2,1,0:T(8,128)} %param.12, f32[16,512,2,64]{1,3,2,0:T(8,128)S(1)} %fusion.20, f32[512]{0:T(512)S(1)} %fusion.50), kind=kOutput, calls=%fused_computation.5 | convolution fusion | flops 6444548096 | bytes 25167872 | tf_op jit(solution)/shard_map/skt,skcl->cstl/dot_general | solution.py:44
  571.4 15.8 %add_bitcast_fusion = (f32[2,16,512,64]{2,3,0,1:T(8,128)}, f32[2,16,512,64]{2,3,0,1:T(8,128)}) fusion(f32[16,2,64,512]{3,2,1,0:T(8,128)} %fusion, f32[16,512,512]{2,1,0:T(8,128)} %param.12, f32[16,512,2,64]{1,3,2,0:T(8,128)S(1)} %fusion.20, f32[512]{0:T(512)S(1)} %fusion.50), kind=kOutput, calls=%fused_computation.36 | convolution fusion | flops 6445596672 | bytes 33556480 | tf_op jit(solution)/shard_map/skt,skcl->cstl/dot_general | solution.py:43
  587.3 7.4 rev.7
  594.7 8.1 pad_maximum_fusion
  602.8 23.1 %copy.90 = f32[2,16,1024,64]{3,0,1,2:T(2,128)} copy(f32[2,16,1024,64]{2,3,0,1:T(8,128)} %pad_maximum_fusion) | data formatting | bytes 16777216 | tf_op jit(solution)/shard_map/concatenate | solution.py:47
  625.9 20.1 %reshape.290 = f32[8,1,262144]{2,1,0:T(1,128)} reshape(f32[1024,16,2,64]{3,2,1,0:T(2,128)} %bitcast.80) | data formatting | bytes 16777216
  646.1 188.7 %all_to_all.70 = f32[8,1,262144]{2,1,0:T(1,128)} all-to-all(f32[8,1,262144]{2,1,0:T(1,128)} %reshape.290), channel_id=1, replica_groups=mesh['band'=8,'lev'=4] {'band'}, dimensions={0} | all-to-all | bytes 16777216 | tf_op jit(solution)/shard_map/all_to_all | solution.py:105
  835.3 26.4 %reduce = f32[8,262144]{1,0:T(8,128)} reduce(f32[8,1,262144]{2,1,0:T(1,128)} %all_to_all.70, f32[]{:T(128)} %broadcast.326), dimensions={1}, to_apply=%all_to_all.58.reduce_sub_computation | reduce | bytes 16777220 | tf_op jit(solution)/shard_map/all_to_all | solution.py:105
  861.7 25.7 %reshape.291 = f32[1024,16,2,64]{3,2,1,0:T(2,128)} reshape(f32[8,262144]{1,0:T(8,128)} %reduce) | data formatting | bytes 16777216
  887.5 17.4 %copy.111 = f32[2,16,8,128,64]{3,1,2,0,4:T(8,128)} copy(f32[2,16,8,128,64]{4,0,1,3,2:T(2,128)} %bitcast.81) | data formatting | bytes 16777216 | tf_op jit(solution)/shard_map/all_to_all | solution.py:105
  904.8 5.6 all-to-all-start.3
  910.5 2.4 scatter_custom_fusion
  913.0 2.4 scatter_custom_fusion.1
  915.4 3.5 gather_fusion
  919.0 84.7 %all-to-all-done.3 = f32[2,128,128,64]{2,1,0,3:T(8,128)} async-done(((f32[2,128,128,64]{2,1,0,3:T(8,128)}), f32[2,128,128,64]{2,1,0,3:T(8,128)}, u32[]{:S(2)}, u32[]{:S(2)}) %all-to-all-start.3) | async-done | bytes 8388640 | tf_op jit(solution)/shard_map/all_to_all | solution.py:104
  1003.6 10.3 copy.95
  1013.9 10.3 reshape.230
  1024.2 13.3 %copy.96 = f32[2,512,2048]{2,0,1:T(2,128)} copy(f32[2,512,2048]{1,2,0:T(8,128)} %reshape.230) | data formatting | bytes 16777216 | tf_op jit(solution)/shard_map/reshape | solution.py:117
  1037.5 22.7 %gather_fusion.2 = f32[512,2,2048]{2,1,0:T(2,128)} fusion(f32[2,512,2048]{2,0,1:T(2,128)} %copy.96, s32[1024]{0:T(1024)S(1)} %pad_clamp_fusion), kind=kCustom, calls=%fused_computation.1.clone | custom fusion | bytes 16779264 | tf_op jit(solution)/shard_map/jit(_take)/gather | solution.py:117
  1060.2 6.4 select_bitcast_fusion
  1066.6 8.3 copy.97
  1074.8 9.3 copy.98
  1084.1 58.1 %fusion.8 = f32[128,16,2048]{2,1,0:T(8,128)} fusion(f32[128,16,1024]{2,1,0:T(8,128)} %bitcast.90, f32[2048,512]{1,0:T(8,128)} %copy-done.4, f32[2048,512]{1,0:T(8,128)} %copy-done.5), kind=kOutput, calls=%fused_computation.17 | convolution fusion | flops 51543801856 | bytes 33554432 | tf_op jit(solution)/shard_map/dot_general | solution.py:119
  (34 shorter events, 2.1 us)
Async XLA Ops:
  0.6 541.8 %copy-start = (f32[64,64]{1,0:T(8,128)S(1)}, f32[64,64]{1,0:T(8,128)}, u32[]{:S(2)}) copy-start(f32[64,64]{1,0:T(8,128)} %param.15) | copy-start | bytes 49156
  0.6 16.5 %copy-start.7 = (s32[512]{0:T(512)S(1)}, s32[512]{0:T(512)}, u32[]{:S(2)}) copy-start(s32[512]{0:T(512)} %param.13) | copy-start | bytes 6148
  17.2 1.9 copy-start.4
  17.2 3.2 copy-start.5
  378.5 6.4 copy-start.8
  378.5 99.3 %all-to-all-start.1 = ((f32[2,64,1024,16]{2,3,0,1:T(8,128)}), f32[2,64,1024,16]{2,3,0,1:T(8,128)}, u32[]{:S(2)}, u32[]{:S(2)}) async-start(f32[2,64,1024,16]{2,3,0,1:T(8,128)} %bitcast.83), calls=%async_computation.1 | async-start | bytes 16777216 | tf_op jit(solution)/shard_map/all_to_all | solution.py:93
  482.0 3.4 copy-start.2
  542.4 7.9 copy-start.6
  542.4 7.9 copy-start.9
  555.4 16.0 %copy-start.3 = (f32[16,512,2,64]{1,3,2,0:T(8,128)}, f32[16,512,2,64]{1,3,2,0:T(8,128)S(1)}, u32[]{:S(2)}) copy-start(f32[16,512,2,64]{1,3,2,0:T(8,128)S(1)} %fusion.20) | copy-start | bytes 12582916
  904.8 98.8 %all-to-all-start.3 = ((f32[2,128,128,64]{2,1,0,3:T(8,128)}), f32[2,128,128,64]{2,1,0,3:T(8,128)}, u32[]{:S(2)}, u32[]{:S(2)}) async-start(f32[2,128,128,64]{2,1,0,3:T(8,128)} %bitcast.82), calls=%async_computation.3 | async-start | bytes 16777216 | tf_op jit(solution)/shard_map/all_to_all | solution.py:104
  1084.1 58.1 %copy-start.1 = (f32[64,64]{1,0:T(8,128)S(1)}, f32[64,64]{1,0:T(8,128)}, u32[]{:S(2)}) copy-start(f32[64,64]{1,0:T(8,128)} %param.15) | copy-start | bytes 49156
where the time goes:
time: 1150 us; the launch traced here: 1140 us
  blocking collectives  379 us (33%)
  local copies, waits for them, and re-layouts  273 us (24%)
  matrix products  212 us (18%)
  waiting for transfers between devices  176 us (15%)
  other arithmetic  89.2 us (8%)
  starting transfers between devices  11.8 us (1%)
    all_to_all x1, blocking collectives, shards(): lax.all_to_all(fourier, 'band', split_axis=1, concat_axis=2, tiled=True)  190 us
    all_to_all x1, blocking collectives, shards(): lax.all_to_all(synthesised, 'band', split_axis=2, concat_axis=1, tiled=True)  189 us
    all_to_all x1, waiting for transfers between devices, shards(): lax.all_to_all(lax.all_to_all(fourier, 'band', split_axis=1, concat_axis=...  91.2 us
    all_to_all x1, waiting for transfers between devices, shards(): lax.all_to_all(lax.all_to_all(synthesised, 'band', split_axis=2, concat_a...  84.7 us
    dot_general x1, matrix products, shards(): lax.dot_general(table, flat, (((0,), (1,)), ((), ())), precision=highest,...  66.8 us
    dot_general x1, matrix products, shards(): lax.dot_general(coeff_rows, table, (((0,), (1,)), ((), ())), precision=hi...  58.1 us
    unnamed x22, local copies, waits for them, and re-layouts  52.5 us
    all_to_all x1, other arithmetic, shards(): lax.all_to_all(synthesised, 'band', split_axis=2, concat_axis=1, tiled=True)  26.4 us
  transfers between devices with their start and end apart: 2, of which 2 were waited for; matrix products, arithmetic and copies ran while one was open for 1% of the time, Pallas kernels for 0%

commit v1 on v0

--- a/solution.py
+++ b/solution.py
@@ -2,6 +2,16 @@
 import jax.numpy as jnp
 from jax import lax
 from jax.sharding import PartitionSpec as P
+
+chunk_resolve = lambda x_part, bus_axis: jnp.concatenate(
+    lax.all_to_all(
+        jnp.stack(jnp.split(x_part, lax.axis_size(bus_axis), axis=1)),
+        bus_axis,
+        split_axis=0,
+        concat_axis=0,
+    ),
+    axis=2,
+)
 
 
 def wave_table(longitudes, count):
@@ -91,11 +101,7 @@
     own_start = (band_at * levels_count + level_at) * slot_rows
     own_waves = lax.dynamic_slice_in_dim(slot_wavenumber, own_start, slot_rows)
     gathered = lax.all_to_all(
-        lax.all_to_all(fourier, "band", split_axis=1, concat_axis=2, tiled=True),
-        "lev",
-        split_axis=1,
-        concat_axis=3,
-        tiled=True,
+        chunk_resolve(fourier, "band"), "lev", split_axis=1, concat_axis=3, tiled=True
     )
     even, odd = fold(gathered)
     analysed = analyse(legendre_north, even, odd)

time: 1150 us -> 1200 us (1.043)
  blocking collectives: 379 us -> 480 us
  waiting for transfers between devices: 176 us -> 91.2 us
  local copies, waits for them, and re-layouts: 273 us -> 304 us
    all_to_all x1 -> x2, blocking collectives: 190 us -> 291 us  [the longest x1 191 us: lax.all_to_all(jnp.stack(jnp.split(x_part, lax.axis_size(bus_axis), axis=...]
    all_to_all x2 -> x1, waiting for transfers between devices: 176 us -> 91.2 us  [shards(): lax.all_to_all(chunk_resolve(fourier, 'band'), 'lev', split_axis=1, conca...]
    another operation x0 -> x2, local copies, waits for them, and re-layouts: none -> 15.7 us  [jnp.stack(jnp.split(x_part, lax.axis_size(bus_axis), axis=1))]
    unnamed x22 -> x31, local copies, waits for them, and re-layouts: 52.5 us -> 65.3 us
  transfers between devices with their start and end apart: 2 -> 1, of which waited for: 2 -> 1; matrix products, arithmetic and copies ran while one was open for 1% -> 0% of each run, Pallas kernels for 0% -> 0%
where the time goes in v1:
time: 1200 us; the launch traced here: 1190 us
  blocking collectives  480 us (40%)
  local copies, waits for them, and re-layouts  304 us (25%)
  matrix products  212 us (18%)
  other arithmetic  95.4 us (8%)
  waiting for transfers between devices  91.2 us (8%)
    all_to_all x1, blocking collectives, lax.all_to_all(jnp.stack(jnp.split(x_part, lax.axis_size(bus_axis), axis=...  191 us
    all_to_all x1, blocking collectives, shards(): lax.all_to_all(synthesised, 'band', split_axis=2, concat_axis=1, tiled=True)  189 us
    all_to_all x1, blocking collectives, shards(): lax.all_to_all(lax.all_to_all(synthesised, 'band', split_axis=2, concat_a...  101 us
    all_to_all x1, waiting for transfers between devices, shards(): lax.all_to_all(chunk_resolve(fourier, 'band'), 'lev', split_axis=1, conca...  91.2 us
    dot_general x1, matrix products, shards(): lax.dot_general(table, flat, (((0,), (1,)), ((), ())), precision=highest,...  67 us
    unnamed x31, local copies, waits for them, and re-layouts  65.3 us
    dot_general x1, matrix products, shards(): lax.dot_general(coeff_rows, table, (((0,), (1,)), ((), ())), precision=hi...  58 us
    all_to_all x1, other arithmetic, shards(): lax.all_to_all(synthesised, 'band', split_axis=2, concat_axis=1, tiled=True)  26.7 us
  transfers between devices with their start and end apart: 1, of which 1 were waited for; matrix products, arithmetic and copies ran while one was open for 0% of the time, Pallas kernels for 0%

profile of v1, /device:TPU:0, one launch (start us, length us, event | category | flops | bytes accessed | tf_op | source)
XLA Modules:
  0.0 1189.8 jit_solution(4107594151273985878)
XLA Ops:
  0.7 17.7 %sine_negate_fusion = (f32[2048,512]{1,0:T(8,128)}, f32[2048,512]{1,0:T(8,128)}) fusion(), kind=kLoop, calls=%fused_computation.40 | loop fusion | flops 15728640 | bytes 8388608 | tf_op jit(solution)/shard_map/neg | solution.py:23
  18.4 2.4 scatter_custom_fusion
  20.9 2.4 scatter_custom_fusion.1
  23.4 3.5 gather_fusion
  28.0 8.6 fusion.10
  36.6 9.2 copy.41
  45.8 11.7 add_multiply_fusion
  57.5 67.0 %fusion.65 = f32[2,512,2048]{2,1,0:T(8,128)} fusion(f32[2,512,2048]{2,1,0:T(8,128)} %bitcast.128, f32[2048,2048,1]{1,0,2:T(8,128)S(1)} %bitcast.126), kind=kOutput, calls=%fused_computation.114 | convolution fusion | flops 51539607552 | bytes 33554432 | tf_op jit(solution)/shard_map/dot_general | solution.py:96
  124.5 15.4 %copy.42 = f32[2,512,2048]{2,0,1:T(2,128)} copy(f32[2,512,2048]{2,1,0:T(8,128)} %fusion.65) | data formatting | bytes 16777216 | tf_op jit(solution)/shard_map/dot_general | solution.py:96
  140.0 22.7 %gather_fusion.1 = f32[512,2,2048]{2,1,0:T(2,128)} fusion(f32[2,512,2048]{2,0,1:T(2,128)} %copy.42, s32[1024]{0:T(1024)S(1)} %get-tuple-element.22), kind=kCustom, calls=%fused_computation.clone | custom fusion | bytes 16779264 | tf_op jit(solution)/shard_map/jit(_take)/gather | solution.py:100
  162.7 8.5 select_bitcast_fusion.1
  171.1 13.1 %copy.43 = f32[2,512,2048]{1,2,0:T(8,128)} copy(f32[2,512,2048]{2,0,1:T(2,128)} %select_bitcast_fusion.1) | data formatting | bytes 16777216 | tf_op jit(solution)/shard_map/jit(_take)/select_n | solution.py:100
  184.3 3.2 fusion.34
  187.5 4.1 fusion.33
  202.2 13.8 %copy.44 = f32[8,2,64,128,16]{3,4,2,1,0:T(8,128)} copy(f32[8,2,64,128,16]{2,4,3,1,0:T(8,128)} %fusion.27) | data formatting | bytes 16777216 | tf_op jit(solution)/shard_map/stack | solution.py:8
  216.0 190.5 %all_to_all.56 = f32[8,2,64,128,16]{3,4,2,1,0:T(8,128)S(1)} all-to-all(f32[8,2,64,128,16]{3,4,2,1,0:T(8,128)} %copy.44), channel_id=1, replica_groups=mesh['band'=8,'lev'=4] {'band'}, dimensions={0} | all-to-all | bytes 16777216 | tf_op jit(solution)/shard_map/all_to_all | solution.py:7
  406.5 8.3 copy.67
  414.8 9.3 reshape.293
  424.0 5.8 all-to-all-start.1
  431.8 91.2 %all-to-all-done.1 = f32[2,64,1024,16]{2,3,0,1:T(8,128)} async-done(((f32[2,64,1024,16]{2,3,0,1:T(8,128)}), f32[2,64,1024,16]{2,3,0,1:T(8,128)}, u32[]{:S(2)}, u32[]{:S(2)}) %all-to-all-start.1) | async-done | bytes 8388640 | tf_op jit(solution)/shard_map/all_to_all | solution.py:103
  522.9 4.2 copy.48
  527.2 3.4 copy-done.3
  530.6 2.5 slice.15
  533.1 7.4 rev.6
  540.5 4.7 slice_subtract_fusion
  545.2 21.0 %fusion.4 = f32[16,2,64,512]{3,2,1,0:T(8,128)S(1)} fusion(f32[16,512,512]{2,1,0:T(8,128)} %param.12, f32[2,16,512,64]{2,3,1,0:T(8,128)S(1)} %get-tuple-element.15), kind=kOutput, calls=%fused_computation.9 | convolution fusion | flops 6442450944 | bytes 25165824 | tf_op jit(solution)/shard_map/skt,cstl->skcl/dot_general | solution.py:42
  566.2 21.6 %fusion.6 = f32[16,2,64,512]{3,2,1,0:T(8,128)S(1)} fusion(f32[16,512,512]{2,1,0:T(8,128)} %param.12, f32[2,16,512,64]{2,3,1,0:T(8,128)S(1)} %get-tuple-element.16), kind=kOutput, calls=%fused_computation.11 | convolution fusion | flops 6442450944 | bytes 25165824 | tf_op jit(solution)/shard_map/skt,cstl->skcl/dot_general | solution.py:41
  587.8 7.9 fusion.16
  595.7 5.0 fusion.20
  600.8 16.0 %fusion = f32[16,2,64,512]{3,2,1,0:T(8,128)} fusion(f32[16,512,512]{2,1,0:T(8,128)} %param.12, f32[16,512,2,64]{1,3,2,0:T(8,128)S(1)} %fusion.20, f32[512]{0:T(512)S(1)} %fusion.58), kind=kOutput, calls=%fused_computation.5 | convolution fusion | flops 6444548096 | bytes 25167872 | tf_op jit(solution)/shard_map/skt,skcl->cstl/dot_general | solution.py:54
  616.8 15.8 %add_bitcast_fusion = (f32[2,16,512,64]{2,3,0,1:T(8,128)}, f32[2,16,512,64]{2,3,0,1:T(8,128)}) fusion(f32[16,2,64,512]{3,2,1,0:T(8,128)} %fusion, f32[16,512,512]{2,1,0:T(8,128)} %param.12, f32[16,512,2,64]{1,3,2,0:T(8,128)S(1)} %fusion.20, f32[512]{0:T(512)S(1)} %fusion.58), kind=kOutput, calls=%fused_computation.35 | convolution fusion | flops 6445596672 | bytes 33556480 | tf_op jit(solution)/shard_map/skt,skcl->cstl/dot_general | solution.py:53
  632.7 7.4 rev.7
  640.1 8.1 pad_maximum_fusion
  648.2 23.1 %copy.51 = f32[2,16,1024,64]{3,0,1,2:T(2,128)} copy(f32[2,16,1024,64]{2,3,0,1:T(8,128)} %pad_maximum_fusion) | data formatting | bytes 16777216 | tf_op jit(solution)/shard_map/concatenate | solution.py:57
  671.3 20.1 %reshape.298 = f32[8,1,262144]{2,1,0:T(1,128)} reshape(f32[1024,16,2,64]{3,2,1,0:T(2,128)} %bitcast.118) | data formatting | bytes 16777216
  691.4 188.7 %all_to_all.57 = f32[8,1,262144]{2,1,0:T(1,128)} all-to-all(f32[8,1,262144]{2,1,0:T(1,128)} %reshape.298), channel_id=1, replica_groups=mesh['band'=8,'lev'=4] {'band'}, dimensions={0} | all-to-all | bytes 16777216 | tf_op jit(solution)/shard_map/all_to_all | solution.py:111
  880.7 26.7 %reduce = f32[8,262144]{1,0:T(8,128)} reduce(f32[8,1,262144]{2,1,0:T(1,128)} %all_to_all.57, f32[]{:T(128)} %broadcast.326), dimensions={1}, to_apply=%all_to_all.45.reduce_sub_computation | reduce | bytes 16777220 | tf_op jit(solution)/shard_map/all_to_all | solution.py:111
  907.3 25.7 %reshape.299 = f32[1024,16,2,64]{3,2,1,0:T(2,128)} reshape(f32[8,262144]{1,0:T(8,128)} %reduce) | data formatting | bytes 16777216
  933.1 17.4 %copy.71 = f32[2,16,8,128,64]{3,1,2,0,4:T(8,128)} copy(f32[2,16,8,128,64]{4,0,1,3,2:T(2,128)} %bitcast.119) | data formatting | bytes 16777216 | tf_op jit(solution)/shard_map/all_to_all | solution.py:111
  950.5 100.6 %all_to_all.58 = f32[2,128,128,64]{2,1,0,3:T(8,128)} all-to-all(f32[2,128,128,64]{2,1,0,3:T(8,128)} %bitcast.120), channel_id=1, replica_groups=mesh['band'=8,'lev'=4] {'lev'}, dimensions={3} | all-to-all | bytes 16777216 | tf_op jit(solution)/shard_map/all_to_all | solution.py:110
  1051.0 10.3 copy.56
  1061.3 10.3 reshape.238
  1071.6 13.3 %copy.57 = f32[2,512,2048]{2,0,1:T(2,128)} copy(f32[2,512,2048]{1,2,0:T(8,128)} %reshape.238) | data formatting | bytes 16777216 | tf_op jit(solution)/shard_map/reshape | solution.py:123
  1084.9 22.7 %gather_fusion.2 = f32[512,2,2048]{2,1,0:T(2,128)} fusion(f32[2,512,2048]{2,0,1:T(2,128)} %copy.57, s32[1024]{0:T(1024)S(1)} %copy-done.7), kind=kCustom, calls=%fused_computation.1.clone | custom fusion | bytes 16779264 | tf_op jit(solution)/shard_map/jit(_take)/gather | solution.py:123
  1107.6 6.4 select_bitcast_fusion
  1114.0 8.3 copy.58
  1122.2 9.3 copy.59
  1131.5 58.0 %fusion.8 = f32[128,16,2048]{2,1,0:T(8,128)} fusion(f32[128,16,1024]{2,1,0:T(8,128)} %bitcast.127, f32[2048,512]{1,0:T(8,128)} %get-tuple-element.19, f32[2048,512]{1,0:T(8,128)} %get-tuple-element.20), kind=kOutput, calls=%fused_computation.16 | convolution fusion | flops 51543801856 | bytes 33554432 | tf_op jit(solution)/shard_map/dot_general | solution.py:125
  (43 shorter events, 14.3 us)
Async XLA Ops:
  0.6 587.2 %copy-start = (f32[64,64]{1,0:T(8,128)S(1)}, f32[64,64]{1,0:T(8,128)}, u32[]{:S(2)}) copy-start(f32[64,64]{1,0:T(8,128)} %param.15) | copy-start | bytes 49156
  0.6 17.7 %copy-start.6 = (s32[512]{0:T(512)S(1)}, s32[512]{0:T(512)}, u32[]{:S(2)}) copy-start(s32[512]{0:T(512)} %param.13) | copy-start | bytes 6148
  184.3 7.3 copy-start.2
  424.0 6.0 copy-start.9
  424.0 98.9 %all-to-all-start.1 = ((f32[2,64,1024,16]{2,3,0,1:T(8,128)}), f32[2,64,1024,16]{2,3,0,1:T(8,128)}, u32[]{:S(2)}, u32[]{:S(2)}) async-start(f32[2,64,1024,16]{2,3,0,1:T(8,128)} %reshape.293), calls=%async_computation.1 | async-start | bytes 16777216 | tf_op jit(solution)/shard_map/all_to_all | solution.py:103
  527.2 3.4 copy-start.3
  587.8 7.9 copy-start.5
  587.8 7.9 copy-start.10
  600.8 16.1 %copy-start.4 = (f32[16,512,2,64]{1,3,2,0:T(8,128)}, f32[16,512,2,64]{1,3,2,0:T(8,128)S(1)}, u32[]{:S(2)}) copy-start(f32[16,512,2,64]{1,3,2,0:T(8,128)S(1)} %fusion.20) | copy-start | bytes 12582916
  1071.6 13.3 %copy-start.7 = (s32[1024]{0:T(1024)S(1)}, s32[1024]{0:T(1024)}, u32[]{:S(2)}) copy-start(s32[1024]{0:T(1024)} %get-tuple-element.21) | copy-start | bytes 12292
  1084.9 22.7 %copy-start.8 = (pred[512]{0:T(512)(128)(4,1)S(1)}, pred[512]{0:T(512)(128)(4,1)}, u32[]{:S(2)}) copy-start(pred[512]{0:T(512)(128)(4,1)} %get-tuple-element.11) | copy-start | bytes 1540
  1131.5 58.0 %copy-start.1 = (f32[64,64]{1,0:T(8,128)S(1)}, f32[64,64]{1,0:T(8,128)}, u32[]{:S(2)}) copy-start(f32[64,64]{1,0:T(8,128)} %param.15) | copy-start | bytes 49156
